TPU v7x, 512 devices: a whole 4x8x8 slice. The times are simulated.
512 devices in a mesh: occ: 128 (over y, z, core), virt: 4 (over x).
Axes of the slice: x: 4, y: 8, z: 8, core: 2. Of those that a mesh axis runs over, the one named last changes fastest.
Arguments:
- factors: bfloat16 [768, 98304], P('virt', 'occ'), may hold values from -1 to 1
- occ_energy: float32 [64], replicated, may hold values from -2 to -0.5
- virt_energy: float32 [768], replicated, may hold values from 0.2 to 3
- pair_table: int32 [256, 2], P('occ'), may hold values from 0 to 63, as said below
- pair_count: int32 [128], P('occ'), may hold values from 0 to 2, as said below
Outputs:
- gamma: float32 [768, 98304], P('virt', 'occ')
Inputs may be any that keep to these rules, and one draw needn't show every extreme that they name: `pair_table`: each row holds two different orbitals. `pair_count`: the counts sum to exactly 128, and some host has exactly 2.
All inputs are finite; a program needn't handle non-finite values.
Results may differ from a plain program's by a relative error of at most 0.0029.
Values may be sent and summed in bfloat16 or wider, within the bound.
A program may use at most 64 MiB of HBM per device.

v0:
```python
import jax
import jax.numpy as jnp
from jax import lax
from jax.sharding import PartitionSpec as P


def laid_out(blocks, dim):
    dims = list(blocks.shape[1:])
    dims[dim] *= blocks.shape[0]
    return jnp.moveaxis(blocks, 0, dim).reshape(dims)


def gather_together(arrays, axis, dims):
    ravelled = jnp.concatenate([a.reshape(-1) for a in arrays])
    lines, at, finished = (lax.all_gather(ravelled, axis), 0, [])
    for a, dim in zip(arrays, dims):
        blocks = lines[:, at : at + a.size].reshape(-1, *a.shape)
        finished.append(laid_out(blocks, dim))
        at += a.size
    return tuple(finished)


def body(factors, occ_energy, virt_energy, pair_table, pair_count):
    tables, counts = gather_together((pair_table, pair_count), "occ", (0, 0))
    hosts_total = lax.axis_size("occ")
    per_host = pair_table.shape[0]
    entries = jnp.arange(hosts_total * per_host, dtype=jnp.int32)
    active = entries % per_host < jnp.repeat(counts, per_host)
    live_total = per_host * hosts_total // 2
    slot_count = -(-live_total // hosts_total)
    ranking = jnp.cumsum(active.astype(jnp.int32)) - 1
    targets = jnp.arange(hosts_total * slot_count, dtype=jnp.int32)
    select = (active[None, :] & (ranking[None, :] == targets[:, None])).astype(jnp.int32)
    plan = jnp.sum(select[:, :, None] * tables[None, :, :], axis=1).reshape(
        hosts_total, slot_count, 2
    )
    enabled = jnp.max(select, axis=1).reshape(hosts_total, slot_count)
    column = lax.axis_index("virt")
    myself = lax.axis_index("occ")
    orbital_count = occ_energy.shape[0]
    slab_width = factors.shape[0]
    aux_local = factors.shape[1] // orbital_count
    slab_energy = lax.dynamic_slice_in_dim(virt_energy, column * slab_width, slab_width)
    source_cube = factors.reshape(factors.shape[0], aux_local, orbital_count)

    def one_slot(position, accumulated):
        orbitals = lax.dynamic_index_in_dim(plan, position, 1, keepdims=False)
        flags = lax.dynamic_index_in_dim(enabled, position, 1, keepdims=False)
        targets_flat = orbitals.T.reshape(-1)
        picked = jnp.take(source_cube, targets_flat, axis=2)
        outgoing = picked.reshape(factors.shape[0], aux_local, 2, hosts_total)
        incoming = lax.all_to_all(outgoing, "occ", split_axis=3, concat_axis=1, tiled=True)
        both = lax.all_gather(incoming, "virt", axis=0, tiled=True)
        left = both[:, :, 0, 0]
        right = both[:, :, 1, 0]
        mine = lax.dynamic_index_in_dim(orbitals, myself, 0, keepdims=False)
        live_here = lax.dynamic_index_in_dim(flags, myself, 0, keepdims=False).astype(jnp.float32)
        left_slab = lax.dynamic_slice_in_dim(left, column * slab_width, slab_width, 0)
        right_slab = lax.dynamic_slice_in_dim(right, column * slab_width, slab_width, 0)
        couple_rows = lax.dot_general(
            left_slab, right, (((1,), (1,)), ((), ())), preferred_element_type=jnp.float32
        )
        couple_cols = lax.dot_general(
            left, right_slab, (((1,), (1,)), ((), ())), preferred_element_type=jnp.float32
        )
        energy_sum = jnp.take(occ_energy, mine[0]) + jnp.take(occ_energy, mine[1])
        ampl_rows = couple_rows / (energy_sum - slab_energy[:, None] - virt_energy[None, :])
        ampl_cols = couple_cols / (energy_sum - virt_energy[:, None] - slab_energy[None, :])
        mixed_rows = ((2.0 * ampl_rows - ampl_cols.T) * live_here).astype(jnp.bfloat16)
        mixed_cols = ((2.0 * ampl_cols - ampl_rows.T) * live_here).astype(jnp.bfloat16)
        toward_first = jnp.dot(mixed_rows, right, preferred_element_type=jnp.float32)
        toward_second = lax.dot_general(
            mixed_cols, left, (((0,), (0,)), ((), ())), preferred_element_type=jnp.float32
        )
        packed = jnp.stack(
            [toward_first.astype(jnp.bfloat16), toward_second.astype(jnp.bfloat16)], axis=2
        )
        packed = packed.reshape(slab_width, hosts_total, aux_local, 2, 1)
        returned = lax.all_to_all(packed, "occ", split_axis=1, concat_axis=4, tiled=True)
        onehot = (
            targets_flat[:, None] == jnp.arange(orbital_count, dtype=jnp.int32)[None, :]
        ).astype(jnp.bfloat16)
        added = jnp.dot(
            returned.reshape(slab_width * aux_local, 2 * hosts_total),
            onehot,
            preferred_element_type=jnp.float32,
        )
        return accumulated + added.reshape(accumulated.shape)

    start = jnp.zeros(factors.shape, jnp.float32)
    return lax.fori_loop(0, slot_count, one_slot, start)


def solution(mesh):
    in_specs = (P("virt", "occ"), P(), P(), P("occ", None), P("occ"))
    out_specs = P("virt", "occ")
    return jax.shard_map(body, mesh=mesh, in_specs=in_specs, out_specs=out_specs, check_vma=False)
```

profile of v0, /device:TPU:8, one launch (start us, length us, event | category | flops | bytes accessed | tf_op | source)
XLA Modules:
  0.0 244.5 jit_solution(16003386581368237176)
XLA Ops:
  6.5 1.1 copy.56
  8.5 0.8 reshape.178
  9.3 1.3 dynamic-slice.11
  11.4 31.4 %all-reduce = s32[640]{0:T(1024)S(1)} all-reduce(s32[640]{0:T(1024)S(1)} %add_dynamic-update-slice_fusion), channel_id=2, replica_groups=mesh['occ'=128,'virt'=4] {'occ'}, use_global_device_ids=true, to_apply=%add | all-reduce | flops 640 | bytes 5120
  43.7 0.3 reduce-window.9
  44.8 0.8 gather_fusion
  45.5 2.8 %copy.69 = bf16[192,12,2,128]{3,2,0,1:T(2,128)(2,1)} copy(bf16[192,12,2,128]{0,1,3,2:T(8,128)(2,1)S(1)} %bitcast.73) | data formatting | bytes 2359296 | tf_op jit(solution)/shard_map/while/body/eval_jaxpr/jit(_take)/gather | solution.py:50
  48.3 2.3 broadcast_select_fusion
  50.6 3.2 %copy.59 = bf16[192,12,2,128]{0,2,1,3:T(2,128)(2,1)S(1)} copy(bf16[192,12,2,128]{3,2,0,1:T(2,128)(2,1)S(1)} %broadcast_select_fusion) | data formatting | bytes 2359296 | tf_op jit(solution)/shard_map/while/body/eval_jaxpr/jit(_take)/select_n | solution.py:50
  53.8 48.7 %all_to_all.41 = bf16[192,12,2,128]{0,2,1,3:T(2,128)(2,1)S(1)} all-to-all(bf16[192,12,2,128]{0,2,1,3:T(2,128)(2,1)S(1)} %copy.59), channel_id=1, replica_groups=mesh['occ'=128,'virt'=4] {'occ'}, dimensions={3} | all-to-all | bytes 2359296 | tf_op jit(solution)/shard_map/while/body/eval_jaxpr/all_to_all | solution.py:52
  102.5 4.4 %copy.60 = bf16[192,1536,2,1]{1,2,3,0:T(2,128)(2,1)} copy(bf16[192,1536,2,1]{0,2,1,3:T(2,128)(2,1)S(1)} %bitcast.74) | data formatting | bytes 2359296 | tf_op jit(solution)/shard_map/while/body/eval_jaxpr/all_to_all | solution.py:52
  107.0 0.6 fusion.44
  111.7 0.6 dynamic_slice.37
  113.0 0.6 fusion.45
  114.9 43.6 %all-gather.3.cloned.1.call-done = bf16[768,1536,2,1]{1,2,3,0:T(2,128)(2,1)} async-done(((bf16[192,1536,2,1]{1,2,3,0:T(2,128)(2,1)}), bf16[768,1536,2,1]{1,2,3,0:T(2,128)(2,1)}) %all-gather.3.cloned.1.call-update) | async-done | bytes 4718608 | tf_op jit(solution)/shard_map/while/body/eval_jaxpr/all_gather | solution.py:53
  158.5 9.6 %fusion.43 = (bf16[768,1536,1,1]{1,2,3,0:T(2,128)(2,1)S(1)}, bf16[768,1536,1,1]{1,2,3,0:T(2,128)(2,1)S(1)}) fusion(bf16[768,1536,2,1]{1,2,3,0:T(2,128)(2,1)} %all-gather.3.cloned.1.call-done), kind=kLoop, calls=%fused_computation.67 | loop fusion | bytes 9437184 | tf_op jit(solution)/shard_map/while/body/eval_jaxpr/slice | solution.py:55
  168.2 0.6 copy.70
  168.8 0.6 copy.71
  169.4 0.9 fusion.4
  170.3 0.9 fusion.1
  171.2 0.8 convolution_convert_fusion
  172.0 0.8 convolution_convert_fusion.1
  172.8 0.3 copy.64
  173.1 0.2 stack.13
  173.3 0.3 copy.63
  173.6 0.2 stack.12
  173.8 0.4 pad_maximum_fusion
  174.3 2.4 copy.65
  176.7 56.3 %all_to_all.42 = bf16[192,128,12,2,1]{0,3,4,2,1:T(2,128)(2,1)S(1)} all-to-all(bf16[192,128,12,2,1]{0,3,4,2,1:T(2,128)(2,1)S(1)} %copy.65), channel_id=1, replica_groups=mesh['occ'=128,'virt'=4] {'occ'}, dimensions={1} | all-to-all | bytes 2359296 | tf_op jit(solution)/shard_map/while/body/eval_jaxpr/all_to_all | solution.py:79
  233.0 2.9 %copy.66 = bf16[192,1,12,2,128,1]{4,3,2,0,5,1:T(2,128)(2,1)S(1)} copy(bf16[192,1,12,2,128,1]{0,3,2,4,5,1:T(2,128)(2,1)S(1)} %bitcast.75) | data formatting | bytes 2359296 | tf_op jit(solution)/shard_map/while/body/eval_jaxpr/all_to_all | solution.py:79
  236.0 0.5 fusion.6
  236.5 1.1 reshape.186
  (33 shorter events, 2.3 us)
Async XLA Ops:
  6.5 152.0 %all-gather.3.cloned.1.call-start = ((), (), s32[]{:S(2)}) async-start(), calls=%async_computation.2 | async-start | bytes 5898240 | tf_op jit(solution)/shard_map/while/body/eval_jaxpr/all_gather | solution.py:53
  102.5 10.5 %copy-start.1 = (f32[64]{0:T(128)S(1)}, f32[64]{0:T(128)}, u32[]{:S(2)}) copy-start(f32[64]{0:T(128)} %param.6) | copy-start | bytes 772
  102.5 12.3 %copy-start = (f32[768]{0:T(1024)S(1)}, f32[768]{0:T(1024)}, u32[]{:S(2)}) copy-start(f32[768]{0:T(1024)} %param.7) | copy-start | bytes 9220
Sparse Core Ops, SparseCore 0:
  107.0 51.4 all-gather.2
where the time goes:
time: 245 us; the launch traced here: 244 us
  blocking collectives  136 us (56%)
  waiting for transfers between devices  43.6 us (18%)
  local copies, waits for them, and re-layouts  36 us (15%)
  between operations  20.8 us (8%)
  matrix products  3.96 us (2%)
  other arithmetic  3.7 us (2%)
    all_to_all x1, blocking collectives, one_slot(): lax.all_to_all(packed, 'occ', split_axis=1, concat_axis=4, tiled=True)  56.3 us
    all_to_all x1, blocking collectives, one_slot(): lax.all_to_all(outgoing, 'occ', split_axis=3, concat_axis=1, tiled=True)  48.7 us
    all_gather x1, waiting for transfers between devices, one_slot(): both = lax.all_gather(incoming, 'virt', axis=0, tiled=True)  43.6 us
    unnamed x1, blocking collectives  31.4 us
    slice x1, local copies, waits for them, and re-layouts, one_slot(): right = both[:, :, 1, 0]  9.63 us
  transfers between devices with their start and end apart: 1, of which 1 were waited for; matrix products, arithmetic and copies ran while one was open for 1% of the time, Pallas kernels for 0%

commit v1 on v0

--- a/solution.py
+++ b/solution.py
@@ -2,6 +2,15 @@
 import jax.numpy as jnp
 from jax import lax
 from jax.sharding import PartitionSpec as P
+from jax.lax import axis_index, ppermute, psum
+
+
+def reach_widths(shard_in, where_dim):
+    shard_in = jnp.moveaxis(shard_in, 0, where_dim)
+    small = shard_in.shape
+    return shard_in.reshape(
+        *small[:where_dim], small[where_dim] * small[where_dim + 1], *small[where_dim + 2 :]
+    )
 
 
 def laid_out(blocks, dim):
@@ -50,7 +59,27 @@
         picked = jnp.take(source_cube, targets_flat, axis=2)
         outgoing = picked.reshape(factors.shape[0], aux_local, 2, hosts_total)
         incoming = lax.all_to_all(outgoing, "occ", split_axis=3, concat_axis=1, tiled=True)
-        both = lax.all_gather(incoming, "virt", axis=0, tiled=True)
+        n = psum(1, "virt")
+        stack_in = []
+        for src_i in range(n):
+            stack_in.append((src_i, (src_i + 1) % n))
+        views = []
+        for jj, m in stack_in:
+            views.append((m, jj))
+        v_now, kept_arr = ([], [])
+        for kk in range(n - 1):
+            if kk % 2 == 0:
+                v_now.append(
+                    ppermute(v_now[-1] if v_now else incoming, axis_name="virt", perm=stack_in)
+                )
+            else:
+                kept_arr.append(
+                    ppermute(kept_arr[-1] if kept_arr else incoming, axis_name="virt", perm=views)
+                )
+        oldest = jnp.stack([*v_now[::-1], incoming, *kept_arr], axis=0)
+        f_next = axis_index("virt") - len(v_now)
+        oldest = oldest[(jnp.arange(n) - f_next) % n]
+        both = reach_widths(oldest, 0)
         left = both[:, :, 0, 0]
         right = both[:, :, 1, 0]
         mine = lax.dynamic_index_in_dim(orbitals, myself, 0, keepdims=False)

time: 245 us -> 231 us (0.943)
  between operations: 20.8 us -> 7.22 us
  starting transfers between devices: 0.01 us -> 9.4 us
  waiting for transfers between devices: 43.6 us -> 35.1 us
  other arithmetic: 3.7 us -> 7.47 us
  local copies, waits for them, and re-layouts: 36 us -> 33.5 us
    all_gather x1 -> x0, waiting for transfers between devices: 43.6 us -> none  [one_slot(): both = lax.all_gather(incoming, 'virt', axis=0, tiled=True)]
    ppermute x0 -> x3, waiting for transfers between devices: none -> 35.1 us  [the longest x2 35.1 us: one_slot(): ppermute(v_now[-1] if v_now else incoming, axis_name='virt', perm=stack_in)]
    ppermute x0 -> x3, starting transfers between devices: none -> 9.4 us  [the longest x2 5.76 us: one_slot(): ppermute(v_now[-1] if v_now else incoming, axis_name='virt', perm=stack_in)]
    slice x1, local copies, waits for them, and re-layouts: 9.63 us -> 0.31 us  [one_slot(): right = both[:, :, 1, 0]]
    gather x0 -> x2, local copies, waits for them, and re-layouts: none -> 7.99 us  [one_slot(): oldest = oldest[(jnp.arange(n) - f_next) % n]]
    another operation x2 -> x3, other arithmetic: 0.35 us -> 4.18 us  [the longest x1 3.83 us: one_slot(): oldest = jnp.stack([*v_now[::-1], incoming, *kept_arr], axis=0)]
    all_to_all x1, blocking collectives: 56.3 us -> 53.5 us  [one_slot(): lax.all_to_all(packed, 'occ', split_axis=1, concat_axis=4, tiled=True)]
  transfers between devices with their start and end apart: 1 -> 3, of which waited for: 1 -> 2; matrix products, arithmetic and copies ran while one was open for 1% -> 3% of each run, Pallas kernels for 0% -> 0%
where the time goes in v1:
time: 231 us; the launch traced here: 230 us
  blocking collectives  134 us (58%)
  waiting for transfers between devices  35.1 us (15%)
  local copies, waits for them, and re-layouts  33.5 us (15%)
  starting transfers between devices  9.4 us (4%)
  other arithmetic  7.47 us (3%)
  between operations  7.22 us (3%)
  matrix products  3.98 us (2%)
    all_to_all x1, blocking collectives, one_slot(): lax.all_to_all(packed, 'occ', split_axis=1, concat_axis=4, tiled=True)  53.5 us
    all_to_all x1, blocking collectives, one_slot(): lax.all_to_all(outgoing, 'occ', split_axis=3, concat_axis=1, tiled=True)  48.7 us
    ppermute x2, waiting for transfers between devices, one_slot(): ppermute(v_now[-1] if v_now else incoming, axis_name='virt', perm=stack_in)  35.1 us
    unnamed x1, blocking collectives  31.4 us
    gather x2, local copies, waits for them, and re-layouts, one_slot(): oldest = oldest[(jnp.arange(n) - f_next) % n]  7.99 us
    ppermute x2, starting transfers between devices, one_slot(): ppermute(v_now[-1] if v_now else incoming, axis_name='virt', perm=stack_in)  5.76 us
  transfers between devices with their start and end apart: 3, of which 2 were waited for; matrix products, arithmetic and copies ran while one was open for 3% of the time, Pallas kernels for 0%

profile of v1, /device:TPU:8, one launch (start us, length us, event | category | flops | bytes accessed | tf_op | source)
XLA Modules:
  0.0 230.3 jit_solution(18121859408664538437)
XLA Ops:
  0.7 0.8 reshape.232
  1.4 1.3 dynamic-slice.11
  3.5 31.4 %all-reduce = s32[640]{0:T(1024)S(1)} all-reduce(s32[640]{0:T(1024)S(1)} %add_dynamic-update-slice_fusion), channel_id=2, replica_groups=mesh['occ'=128,'virt'=4] {'occ'}, use_global_device_ids=true, to_apply=%add | all-reduce | flops 640 | bytes 5120
  36.9 1.1 copy.69
  38.2 0.8 gather_fusion
  39.0 2.1 copy.85
  41.1 1.0 broadcast_select_fusion
  42.1 3.2 %copy.72 = bf16[192,12,2,128]{0,2,1,3:T(2,128)(2,1)S(1)} copy(bf16[192,12,2,128]{3,2,0,1:T(2,128)(2,1)S(1)} %broadcast_select_fusion) | data formatting | bytes 2359296 | tf_op jit(solution)/shard_map/while/body/eval_jaxpr/jit(_take)/select_n | solution.py:59
  45.3 48.7 %all_to_all.41 = bf16[192,12,2,128]{0,2,1,3:T(2,128)(2,1)S(1)} all-to-all(bf16[192,12,2,128]{0,2,1,3:T(2,128)(2,1)S(1)} %copy.72), channel_id=1, replica_groups=mesh['occ'=128,'virt'=4] {'occ'}, dimensions={3} | all-to-all | bytes 2359296 | tf_op jit(solution)/shard_map/while/body/eval_jaxpr/all_to_all | solution.py:61
  94.0 1.1 copy.73
  95.1 3.4 %collective-permute-start = (bf16[192,1536,2,1]{1,0,2,3:T(8,128)(2,1)S(1)}, bf16[192,1536,2,1]{1,0,2,3:T(8,128)(2,1)}, u32[]{:S(2)}, u32[]{:S(2)}) collective-permute-start(bf16[192,1536,2,1]{1,0,2,3:T(8,128)(2,1)S(1)} %copy.73), channel_id=1, source_target_pairs={{0,1},{1,2},{2,3},{3,0},{4,5},{5,6},{6,7},{7,4},{8,9},{9,10},{10,1... | collective-permute-start | bytes 3538952 | tf_op jit(solution)/shard_map/while/body/eval_jaxpr/ppermute | solution.py:73
  98.5 2.9 %copy.74 = bf16[192,1536,2,1]{1,0,3,2:T(8,128)(2,1)} copy(bf16[192,1536,2,1]{0,2,1,3:T(2,128)(2,1)S(1)} %bitcast.88) | data formatting | bytes 2359296 | tf_op jit(solution)/shard_map/while/body/eval_jaxpr/all_to_all | solution.py:61
  101.5 3.6 %collective-permute-start.2 = (bf16[192,1536,2,1]{1,0,3,2:T(8,128)(2,1)}, bf16[192,1536,2,1]{1,0,3,2:T(8,128)(2,1)}, u32[]{:S(2)}, u32[]{:S(2)}) collective-permute-start(bf16[192,1536,2,1]{1,0,3,2:T(8,128)(2,1)} %copy.74), channel_id=1, source_target_pairs={{1,0},{2,1},{3,2},{0,3},{5,4},{6,5},{7,6},{4,7},{9,8},{10,9},{11,1... | collective-permute-start | bytes 3538952 | tf_op jit(solution)/shard_map/while/body/eval_jaxpr/ppermute | solution.py:77
  105.1 19.0 %collective-permute-done = bf16[192,1536,2,1]{1,0,2,3:T(8,128)(2,1)} collective-permute-done((bf16[192,1536,2,1]{1,0,2,3:T(8,128)(2,1)S(1)}, bf16[192,1536,2,1]{1,0,2,3:T(8,128)(2,1)}, u32[]{:S(2)}, u32[]{:S(2)}) %collective-permute-start) | collective-permute-done | bytes 1179680 | tf_op jit(solution)/shard_map/while/body/eval_jaxpr/ppermute | solution.py:73
  124.1 2.4 %collective-permute-start.1 = (bf16[192,1536,2,1]{1,0,2,3:T(8,128)(2,1)}, bf16[192,1536,2,1]{1,0,2,3:T(8,128)(2,1)}, u32[]{:S(2)}, u32[]{:S(2)}) collective-permute-start(bf16[192,1536,2,1]{1,0,2,3:T(8,128)(2,1)} %collective-permute-done), channel_id=1, source_target_pairs={{0,1},{1,2},{2,3},{3,0},{4,5},{5,6},{6,7},{7,4},{8,9},{9,10},{10,1... | collective-permute-start | bytes 3538952 | tf_op jit(solution)/shard_map/while/body/eval_jaxpr/ppermute | solution.py:73
  130.9 0.6 dynamic_slice.37
  132.1 0.7 fusion.51
  134.0 0.7 broadcast_subtract_fusion.1
  134.7 0.6 broadcast_subtract_fusion
  135.3 1.1 copy.76
  136.5 16.0 %collective-permute-done.1 = bf16[192,1536,2,1]{1,0,2,3:T(8,128)(2,1)} collective-permute-done((bf16[192,1536,2,1]{1,0,2,3:T(8,128)(2,1)}, bf16[192,1536,2,1]{1,0,2,3:T(8,128)(2,1)}, u32[]{:S(2)}, u32[]{:S(2)}) %collective-permute-start.1) | collective-permute-done | bytes 1179680 | tf_op jit(solution)/shard_map/while/body/eval_jaxpr/ppermute | solution.py:73
  152.5 3.8 %maximum_bitcast_fusion = bf16[4,192,1536,2]{2,1,3,0:T(8,128)(2,1)} fusion(bf16[1,192,1536,2,1]{2,1,3,0,4:T(8,128)(2,1)} %bitcast.19, bf16[1,192,1536,2,1]{2,1,3,0,4:T(8,128)(2,1)S(1)} %copy.76, bf16[1,192,1536,2,1]{2,1,3,0,4:T(8,128)(2,1)} %bitcast.14, bf16[1,192,1536,2,1]{2,1,3,0,4:T(8,128)(2,1)} %bitcast.13), kind=kLoop, calls=%fused_computation.2 | loop fusion | flops 7077888 | bytes 9437184 | tf_op jit(solution)/shard_map/while/body/eval_jaxpr/stack | solution.py:79
  156.3 5.4 %gather_fusion.1 = bf16[4,192,1536,2]{2,1,3,0:T(8,128)(2,1)} fusion(bf16[4,192,1536,2]{2,1,3,0:T(8,128)(2,1)} %maximum_bitcast_fusion, s32[1024]{0:T(1024)S(1)} %pad_clamp_fusion), kind=kCustom, calls=%fused_computation.1 | custom fusion | bytes 9437200 | tf_op jit(solution)/shard_map/while/body/eval_jaxpr/gather | solution.py:81
  161.7 2.6 %copy.78 = bf16[4,192,1536,2]{2,1,0,3:T(8,128)(2,1)S(1)} copy(bf16[4,192,1536,2]{2,1,3,0:T(8,128)(2,1)} %gather_fusion.1) | data formatting | bytes 9437184 | tf_op jit(solution)/shard_map/while/body/eval_jaxpr/gather | solution.py:81
  164.6 0.9 fusion.1
  165.6 0.9 fusion.4
  166.5 0.8 convolution_convert_fusion.1
  167.4 0.8 convolution_convert_fusion
  169.7 2.4 %copy.81 = bf16[192,128,12,2,1]{0,3,4,2,1:T(2,128)(2,1)S(1)} copy(bf16[192,128,12,2,1]{0,2,1,4,3:T(8,128)(2,1)S(1)} %pad_maximum_fusion) | data formatting | bytes 2359296 | tf_op jit(solution)/shard_map/while/body/eval_jaxpr/stack | solution.py:104
  172.1 53.5 %all_to_all.42 = bf16[192,128,12,2,1]{0,3,4,2,1:T(2,128)(2,1)S(1)} all-to-all(bf16[192,128,12,2,1]{0,3,4,2,1:T(2,128)(2,1)S(1)} %copy.81), channel_id=1, replica_groups=mesh['occ'=128,'virt'=4] {'occ'}, dimensions={1} | all-to-all | bytes 2359296 | tf_op jit(solution)/shard_map/while/body/eval_jaxpr/all_to_all | solution.py:108
  225.7 2.9 %copy.82 = bf16[192,1,12,2,128,1]{4,3,2,0,5,1:T(2,128)(2,1)S(1)} copy(bf16[192,1,12,2,128,1]{0,3,2,4,5,1:T(2,128)(2,1)S(1)} %bitcast.96) | data formatting | bytes 2359296 | tf_op jit(solution)/shard_map/while/body/eval_jaxpr/all_to_all | solution.py:108
  229.1 1.1 reshape.241
  (53 shorter events, 5.3 us)
Async XLA Ops:
  36.8 89.7 %copy-start = (s32[128,2]{0,1:T(2,128)}, s32[128,2]{0,1:T(2,128)S(1)}, u32[]{:S(2)}) copy-start(s32[128,2]{0,1:T(2,128)S(1)} %multiply_reduce_fusion) | copy-start | bytes 3076
  94.0 38.1 %copy-start.5 = (f32[64]{0:T(128)S(1)}, f32[64]{0:T(128)}, u32[]{:S(2)}) copy-start(f32[64]{0:T(128)} %param.6) | copy-start | bytes 772
  94.0 40.0 %copy-start.2 = (f32[768]{0:T(1024)S(1)}, f32[768]{0:T(1024)}, u32[]{:S(2)}) copy-start(f32[768]{0:T(1024)} %param.7) | copy-start | bytes 9220
  95.1 29.0 %collective-permute-start = (bf16[192,1536,2,1]{1,0,2,3:T(8,128)(2,1)S(1)}, bf16[192,1536,2,1]{1,0,2,3:T(8,128)(2,1)}, u32[]{:S(2)}, u32[]{:S(2)}) collective-permute-start(bf16[192,1536,2,1]{1,0,2,3:T(8,128)(2,1)S(1)} %copy.73), channel_id=1, source_target_pairs={{0,1},{1,2},{2,3},{3,0},{4,5},{5,6},{6,7},{7,4},{8,9},{9,10},{10,1... | collective-permute-start | bytes 3538952 | tf_op jit(solution)/shard_map/while/body/eval_jaxpr/ppermute | solution.py:73
  101.5 35.0 %collective-permute-start.2 = (bf16[192,1536,2,1]{1,0,3,2:T(8,128)(2,1)}, bf16[192,1536,2,1]{1,0,3,2:T(8,128)(2,1)}, u32[]{:S(2)}, u32[]{:S(2)}) collective-permute-start(bf16[192,1536,2,1]{1,0,3,2:T(8,128)(2,1)} %copy.74), channel_id=1, source_target_pairs={{1,0},{2,1},{3,2},{0,3},{5,4},{6,5},{7,6},{4,7},{9,8},{10,9},{11,1... | collective-permute-start | bytes 3538952 | tf_op jit(solution)/shard_map/while/body/eval_jaxpr/ppermute | solution.py:77
  124.1 28.3 %collective-permute-start.1 = (bf16[192,1536,2,1]{1,0,2,3:T(8,128)(2,1)}, bf16[192,1536,2,1]{1,0,2,3:T(8,128)(2,1)}, u32[]{:S(2)}, u32[]{:S(2)}) collective-permute-start(bf16[192,1536,2,1]{1,0,2,3:T(8,128)(2,1)} %collective-permute-done), channel_id=1, source_target_pairs={{0,1},{1,2},{2,3},{3,0},{4,5},{5,6},{6,7},{7,4},{8,9},{9,10},{10,1... | collective-permute-start | bytes 3538952 | tf_op jit(solution)/shard_map/while/body/eval_jaxpr/ppermute | solution.py:73
  165.5 1.0 copy-start.3
  165.6 1.0 copy-start.4
  165.6 1.0 copy-start.6
  165.6 1.0 copy-start.7
  172.1 56.5 %copy-start.1 = (s32[128,2]{0,1:T(2,128)S(1)}, s32[128,2]{0,1:T(2,128)}, u32[]{:S(2)}) copy-start(s32[128,2]{0,1:T(2,128)} %copy-done) | copy-start | bytes 3076
